TPU v7x, 32 devices: a whole 2x2x4 slice. The times are simulated.
32 devices in a mesh: blk: 8 (over z, y), rep: 4 (over x, core).
Axes of the slice: x: 2, y: 2, z: 4, core: 2. Of those that a mesh axis runs over, the one named last changes fastest.
Arguments:
- embeddings: bfloat16 [1024, 256], P('blk'), may hold values from -21 to 21
- targets: float32 [128, 1024], P('rep', 'blk'), may hold values from -180 to 180
Outputs:
- solution: float32 [128, 1024], P('rep', 'blk')
- residual: float32 [128, 1024], P('rep', 'blk')
All inputs are finite; a program needn't handle non-finite values.
Results may differ from a plain program's by a relative error of at most 0.0003.
Values may be sent and summed in bfloat16 or wider, within the bound.
A program may use at most 64 MiB of HBM per device.

v0:
```python
import jax
import jax.numpy as jnp
from jax import lax
from jax.sharding import PartitionSpec as P

ITERS = 2
length_scale = 1.0
noise_var = 1.0


def squared_norms(points):
    widened = points.astype(jnp.float32)
    return jnp.sum(widened * widened, axis=1)


def kernel_tile(own_points, own_norms, own_labels, far_points, far_norms, far_labels):
    products = jnp.einsum("pd,qd->pq", own_points, far_points, preferred_element_type=jnp.float32)
    distance_sq = own_norms[:, None] + far_norms[None, :] - 2.0 * products
    distance_sq = jnp.where(own_labels[:, None] == far_labels[None, :], 0.0, distance_sq)
    return jnp.exp(-jnp.sqrt(distance_sq) / length_scale)


def paired(residual, image):
    return lax.psum((jnp.sum(residual * residual), jnp.sum(residual * image)), ("blk", "rep"))


def per_device(embeddings, targets):
    block_id = lax.axis_index("blk")
    local_count = embeddings.shape[0]
    own_norms = squared_norms(embeddings)
    own_labels = block_id * local_count + jnp.arange(local_count, dtype=jnp.int32)
    everyone = lax.all_gather(embeddings, "blk", axis=0, tiled=True)
    every_norms = squared_norms(everyone)

    def folded_image(direction):
        piece = lax.all_gather(direction, "blk", axis=1, tiled=True)
        count = piece.shape[1]
        far_labels = jnp.arange(count, dtype=jnp.int32)
        tile = kernel_tile(embeddings, own_norms, own_labels, everyone, every_norms, far_labels)
        total = jnp.einsum(
            "rq,pq->rp",
            piece,
            tile,
            precision=lax.Precision.HIGHEST,
            preferred_element_type=jnp.float32,
        )
        return total + noise_var * direction

    solution = jnp.zeros_like(targets)
    residual = targets
    image = folded_image(residual)
    norm_now, product = paired(residual, image)
    alpha = norm_now / product
    direction = residual
    along = image
    for iteration in range(ITERS):
        solution = solution + alpha * direction
        residual = residual - alpha * along
        if iteration + 1 < ITERS:
            image = folded_image(residual)
            norm_next, product = paired(residual, image)
            ratio = norm_next / norm_now
            alpha = norm_next / (product - ratio * norm_next / alpha)
            direction = residual + ratio * direction
            along = image + ratio * along
            norm_now = norm_next
    return (solution, residual)


def solution(mesh):
    in_specs = (P("blk", None), P("rep", "blk"))
    out_specs = (P("rep", "blk"), P("rep", "blk"))
    return jax.shard_map(
        per_device, mesh=mesh, in_specs=in_specs, out_specs=out_specs, check_vma=False
    )
```

profile of v0, /device:TPU:14, one launch (start us, length us, event | category | flops | bytes accessed | tf_op | source)
XLA Modules:
  0.0 184.3 jit_solution(12723505699822419723)
XLA Ops:
  0.6 29.7 %all_gather.9 = bf16[1024,256]{1,0:T(8,128)(2,1)S(1)} all-gather(bf16[128,256]{1,0:T(8,128)(2,1)} %param.2), channel_id=1, replica_groups=mesh['blk'=8,'rep'=4] {'blk'}, dimensions={0}, use_global_device_ids=true | all-gather | bytes 589824 | tf_op jit(solution)/shard_map/all_gather | solution.py:32
  30.3 0.0 copy-start.1
  30.3 0.2 multiply_reduce_fusion
  30.5 0.6 copy-done.1
  31.1 0.1 multiply_reduce_fusion.1
  31.2 0.0 copy-start
  31.2 0.5 fusion.4
  31.7 0.3 copy-done
  32.0 30.0 %all_gather.10 = f32[32,1024]{1,0:T(8,128)S(1)} all-gather(f32[32,128]{1,0:T(8,128)S(1)} %copy-done), channel_id=1, replica_groups=mesh['blk'=8,'rep'=4] {'blk'}, dimensions={1}, use_global_device_ids=true | all-gather | bytes 147456 | tf_op jit(solution)/shard_map/all_gather | solution.py:36
  62.0 1.2 multiply_reduce_fusion.4
  63.2 43.1 %all-reduce.1 = (f32[]{:T(128)}, f32[]{:T(128)}) all-reduce(f32[]{:T(128)} %get-tuple-element.5, f32[]{:T(128)} %get-tuple-element.4), channel_id=1, replica_groups=mesh['blk'=8,'rep'=4] {'blk','rep'}, use_global_device_ids=true, to_apply=%region_1.0 | all-reduce | flops 2 | bytes 16 | tf_op jit(solution)/shard_map/psum | solution.py:24
  107.7 25.4 %all_gather.11 = f32[32,1024]{1,0:T(8,128)S(1)} all-gather(f32[32,128]{1,0:T(8,128)S(1)} %multiply_subtract_fusion.1), channel_id=1, replica_groups=mesh['blk'=8,'rep'=4] {'blk'}, dimensions={1}, use_global_device_ids=true | all-gather | bytes 147456 | tf_op jit(solution)/shard_map/all_gather | solution.py:36
  133.1 1.3 multiply_reduce_fusion.2
  134.4 44.7 %all-reduce = (f32[]{:T(128)}, f32[]{:T(128)}) all-reduce(f32[]{:T(128)} %get-tuple-element.3, f32[]{:T(128)} %get-tuple-element.2), channel_id=1, replica_groups=mesh['blk'=8,'rep'=4] {'blk','rep'}, use_global_device_ids=true, to_apply=%region_7.8 | all-reduce | flops 2 | bytes 16 | tf_op jit(solution)/shard_map/psum | solution.py:24
  183.7 0.6 multiply_subtract_fusion
  (2 shorter events, 0.0 us)
Async XLA Ops:
  30.3 0.8 copy-start.1
  31.2 0.7 copy-start
where the time goes:
time: 185 us; the launch traced here: 184 us
  blocking collectives  173 us (94%)
  between operations  6.58 us (4%)
  matrix products  2.96 us (2%)
    psum x2, blocking collectives, paired(): lax.psum((jnp.sum(residual * residual), jnp.sum(residual * image)), ('blk...  87.8 us
    all_gather x2, blocking collectives, folded_image(): piece = lax.all_gather(direction, 'blk', axis=1, tiled=True)  55.5 us
    all_gather x1, blocking collectives, per_device(): everyone = lax.all_gather(embeddings, 'blk', axis=0, tiled=True)  29.7 us

commit v1 on v0

--- a/solution.py
+++ b/solution.py
@@ -6,6 +6,11 @@
 ITERS = 2
 length_scale = 1.0
 noise_var = 1.0
+
+
+def by_each_axis(array, one, other):
+    half = lax.psum(array, one)
+    return lax.psum(half, other)
 
 
 def squared_norms(points):
@@ -21,7 +26,7 @@
 
 
 def paired(residual, image):
-    return lax.psum((jnp.sum(residual * residual), jnp.sum(residual * image)), ("blk", "rep"))
+    return by_each_axis((jnp.sum(residual * residual), jnp.sum(residual * image)), "rep", "blk")
 
 
 def per_device(embeddings, targets):

time: 185 us -> 159 us (0.86)
  the two profiles are of different devices: /device:TPU:14 before, /device:TPU:0 now
where the time goes in v1:
time: 159 us; the launch traced here: 158 us
  blocking collectives  147 us (92%)
  between operations  6.58 us (4%)
  matrix products  2.94 us (2%)
    all_gather x2, blocking collectives, folded_image(): piece = lax.all_gather(direction, 'blk', axis=1, tiled=True)  61 us
    psum x2, blocking collectives, by_each_axis(): return lax.psum(half, other)  40 us
    all_gather x1, blocking collectives, per_device(): everyone = lax.all_gather(embeddings, 'blk', axis=0, tiled=True)  33.2 us
    psum x2, blocking collectives, by_each_axis(): half = lax.psum(array, one)  12.6 us

profile of v1, /device:TPU:0, one launch (start us, length us, event | category | flops | bytes accessed | tf_op | source)
XLA Modules:
  0.0 158.2 jit_solution(855782369501122017)
XLA Ops:
  0.6 33.2 %all_gather.9 = bf16[1024,256]{1,0:T(8,128)(2,1)S(1)} all-gather(bf16[128,256]{1,0:T(8,128)(2,1)} %param.2), channel_id=1, replica_groups=mesh['blk'=8,'rep'=4] {'blk'}, dimensions={0}, use_global_device_ids=true | all-gather | bytes 589824 | tf_op jit(solution)/shard_map/all_gather | solution.py:37
  33.9 0.0 copy-start.1
  33.9 0.2 multiply_reduce_fusion
  34.1 0.6 copy-done.1
  34.7 0.1 multiply_reduce_fusion.1
  34.8 0.0 copy-start
  34.8 0.5 fusion.4
  35.3 0.3 copy-done
  35.6 30.5 %all_gather.10 = f32[32,1024]{1,0:T(8,128)S(1)} all-gather(f32[32,128]{1,0:T(8,128)S(1)} %copy-done), channel_id=1, replica_groups=mesh['blk'=8,'rep'=4] {'blk'}, dimensions={1}, use_global_device_ids=true | all-gather | bytes 147456 | tf_op jit(solution)/shard_map/all_gather | solution.py:41
  66.1 1.2 multiply_reduce_fusion.4
  67.3 6.3 %all-reduce.3 = (f32[]{:T(128)}, f32[]{:T(128)}) all-reduce(f32[]{:T(128)} %get-tuple-element.5, f32[]{:T(128)} %get-tuple-element.4), channel_id=1, replica_groups=mesh['blk'=8,'rep'=4] {'rep'}, use_global_device_ids=true, to_apply=%region_1.0 | all-reduce | flops 2 | bytes 16 | tf_op jit(solution)/shard_map/psum | solution.py:12
  73.5 22.2 %all-reduce.1 = (f32[]{:T(128)}, f32[]{:T(128)}) all-reduce(f32[]{:T(128)} %get-tuple-element.12, f32[]{:T(128)} %get-tuple-element.13), channel_id=1, replica_groups=mesh['blk'=8,'rep'=4] {'blk'}, use_global_device_ids=true, to_apply=%region_2.3 | all-reduce | flops 2 | bytes 16 | tf_op jit(solution)/shard_map/psum | solution.py:13
  97.0 30.5 %all_gather.11 = f32[32,1024]{1,0:T(8,128)S(1)} all-gather(f32[32,128]{1,0:T(8,128)S(1)} %multiply_subtract_fusion.1), channel_id=1, replica_groups=mesh['blk'=8,'rep'=4] {'blk'}, dimensions={1}, use_global_device_ids=true | all-gather | bytes 147456 | tf_op jit(solution)/shard_map/all_gather | solution.py:41
  127.6 1.3 multiply_reduce_fusion.2
  128.9 6.3 %all-reduce.2 = (f32[]{:T(128)}, f32[]{:T(128)}) all-reduce(f32[]{:T(128)} %get-tuple-element.3, f32[]{:T(128)} %get-tuple-element.2), channel_id=1, replica_groups=mesh['blk'=8,'rep'=4] {'rep'}, use_global_device_ids=true, to_apply=%region_9.10 | all-reduce | flops 2 | bytes 16 | tf_op jit(solution)/shard_map/psum | solution.py:12
  135.2 17.8 %all-reduce = (f32[]{:T(128)}, f32[]{:T(128)}) all-reduce(f32[]{:T(128)} %get-tuple-element.10, f32[]{:T(128)} %get-tuple-element.11), channel_id=1, replica_groups=mesh['blk'=8,'rep'=4] {'blk'}, use_global_device_ids=true, to_apply=%region_10.11 | all-reduce | flops 2 | bytes 16 | tf_op jit(solution)/shard_map/psum | solution.py:13
  157.6 0.6 multiply_subtract_fusion
  (2 shorter events, 0.0 us)
Async XLA Ops:
  33.9 0.8 copy-start.1
  34.8 0.7 copy-start
